TPU v7x, 512 devices: a whole 4x4x16 slice. The times are simulated.
512 devices in a mesh: segment: 4 (over y_lo, core), band: 128 (over z, x, y_hi).
Axes of the slice: x: 4, y: 4 (y_hi: 2, y_lo: 2; y = y_hi * 2 + y_lo), z: 16, core: 2. Of those that a mesh axis runs over, the one named last changes fastest.
Arguments:
- voltages: bfloat16 [2, 2048, 16384], P(None, 'band', 'segment'), may hold values from -6 to 6
- slot_of_antenna: int32 [2048], replicated, may hold values from 0 to 2047, each once
- antenna_positions: int32 [2048, 2], replicated, may hold values from -1000 to 999
- beam_directions: int32 [1024, 2], replicated, may hold values from -64 to 63
Outputs:
- vis_real: float32 [128, 4, 256, 2048], P('band', 'segment')
- vis_imag: float32 [128, 4, 256, 2048], P('band', 'segment')
- beam_series: float32 [2, 4, 128, 2, 16384], P(None, 'segment', 'band')
Inputs may be any that keep to these rules, and one draw needn't show every extreme that they name: `slot_of_antenna`: a permutation of the antennas.
All inputs are finite; a program needn't handle non-finite values.
Results may differ from a plain program's by a relative error of at most 0.005.
Values may be sent and summed in bfloat16 or wider, within the bound.
A program may use at most 64 MiB of HBM per device.

v0:
```python
import math
import jax
import jax.numpy as jnp
from jax import lax
from jax.sharding import PartitionSpec as P

A = 2048
C = 64
BEAMS = 1024
NB = 256


def dft_parts():
    index = jnp.arange(64, dtype=jnp.int32)
    product = jnp.remainder(index[:, None] * index[None, :], 64).astype(jnp.float32)
    theta = product * (2.0 * math.pi / 64.0)
    return (jnp.cos(theta) * 0.125, jnp.sin(theta) * 0.125)


def forward_table():
    cosine, sine = dft_parts()
    return jnp.stack([jnp.stack([cosine, -sine], axis=1), jnp.stack([sine, cosine], axis=1)])


def inverse_table():
    cosine, sine = dft_parts()
    return jnp.stack([jnp.stack([cosine, sine], axis=1), jnp.stack([-sine, cosine], axis=1)])


def channelize(samples):
    count = samples.shape[2] // 64
    values = samples.astype(jnp.float32).reshape(2, samples.shape[1], count, 64)
    spectra = jnp.einsum(
        "pajn,pnqk->kqaj", values, forward_table(), precision=lax.Precision.HIGHEST
    )
    return spectra.astype(jnp.bfloat16)


def paired(spectra):
    doubled = jnp.broadcast_to(spectra[:, None], (spectra.shape[0], 2) + spectra.shape[1:])
    return doubled.reshape((2 * spectra.shape[0],) + spectra.shape[1:])


def steering(channel, directions, positions):
    delay = jnp.remainder(
        directions[:, 0:1] * positions[None, :, 0] + directions[:, 1:2] * positions[None, :, 1], 64
    )
    phase = jnp.remainder(channel * delay, 64).astype(jnp.float32) * (2.0 * math.pi / 64.0)
    return jnp.stack([jnp.cos(phase), -jnp.sin(phase)]).astype(jnp.bfloat16)


def resynthesize(received):
    lanes = received.shape[3]
    beams_here = received.shape[1]
    split = received.reshape(C, 2, beams_here, 2, lanes)
    series = jnp.einsum(
        "khbpj,pkqn->hbqjn", split, inverse_table(), precision=lax.Precision.HIGHEST
    )
    return series.reshape(2, beams_here, 2, lanes * 64)


def per_device(voltages, slot_of_antenna, antenna_positions, beam_directions):
    n_segment = lax.axis_size("segment")
    n_band = lax.axis_size("band")
    segment = lax.axis_index("segment")
    band = lax.axis_index("band")
    pair_count = 2 * C // n_band
    row_block = A // (2 * n_segment)
    beam_block = BEAMS // (2 * n_segment)
    beam_scale = 1.0 / math.sqrt(A)
    pair_ids = band * pair_count + jnp.arange(pair_count, dtype=jnp.int32)
    channels = pair_ids // 2
    halves = pair_ids % 2
    row_starts = (halves * n_segment + segment) * row_block
    beam_starts = halves * (n_segment * beam_block) + segment * beam_block

    def pair_weights(channel, beam_start):
        directions = lax.dynamic_slice_in_dim(beam_directions, beam_start, beam_block, 0)
        return steering(channel, directions, antenna_positions)

    weights = jax.vmap(pair_weights)(channels, beam_starts)

    def pair_terms(block, weight, row_start):
        rows = lax.dynamic_slice_in_dim(block, row_start, row_block, 1)
        turned = jnp.stack([rows[1], -rows[0]])
        left = jnp.stack([rows, turned])
        gram = jnp.einsum("gprt,pat->gra", left, block, preferred_element_type=jnp.float32)
        mixed = jnp.einsum("gba,pat->gbpt", weight, block, preferred_element_type=jnp.float32)
        formed_real = mixed[0, :, 0] - mixed[1, :, 1]
        formed_imag = mixed[0, :, 1] + mixed[1, :, 0]
        return (gram, jnp.stack([formed_real, formed_imag], axis=1) * beam_scale)

    spectra = paired(channelize(voltages))
    owned = lax.all_to_all(spectra, "band", split_axis=0, concat_axis=2, tiled=True)
    ordered = jnp.take(
        lax.all_gather(owned, "segment", axis=3, tiled=True), slot_of_antenna, axis=2
    )
    gram_part, formed_part = jax.vmap(pair_terms)(ordered, weights, row_starts)
    formed_total = formed_part
    gram_total, formed_total = (gram_part, formed_total)
    gram_total = gram_total * (1.0 / NB)
    vis_real = gram_total[:, 0][:, None]
    vis_imag = gram_total[:, 1][:, None]
    series = resynthesize(
        lax.all_to_all(
            formed_total.astype(jnp.bfloat16), "band", split_axis=1, concat_axis=0, tiled=True
        ).astype(formed_total.dtype)
    )
    beam_series = series.reshape(2, 1, series.shape[1], 2, series.shape[3])
    return (vis_real, vis_imag, beam_series)


def solution(mesh):
    in_specs = (P(None, "band", "segment"), P(), P(), P())
    out_specs = (
        P("band", "segment", None, None),
        P("band", "segment", None, None),
        P(None, "segment", "band", None, None),
    )
    return jax.shard_map(
        per_device, mesh=mesh, in_specs=in_specs, out_specs=out_specs, check_vma=False
    )
```

profile of v0, /device:TPU:32, one launch (start us, length us, event | category | flops | bytes accessed | tf_op | source)
XLA Modules:
  0.0 170.9 jit_solution(14214573905199428207)
XLA Ops:
  7.4 0.2 sine_multiply_fusion
  7.5 1.5 reshape.623
  9.0 0.9 fusion.7
  9.9 0.3 copy.34
  10.3 0.2 broadcast_in_dim.34
  10.5 0.6 reshape.700
  11.1 57.2 %all_to_all.27 = bf16[128,2,1024]{2,1,0:T(2,128)(2,1)S(1)} all-to-all(bf16[128,2,1024]{2,1,0:T(2,128)(2,1)S(1)} %reshape.700), channel_id=1, replica_groups=mesh['segment'=4,'band'=128] {'band'}, dimensions={0} | all-to-all | bytes 1048576 | tf_op jit(solution)/shard_map/all_to_all | solution.py:94
  68.2 0.6 reshape.701
  68.9 0.2 copy.35
  69.1 1.3 copy.36
  70.5 5.0 %cosine_convert_fusion = (bf16[1,128,2048]{2,1,0:T(8,128)(2,1)S(1)}, bf16[1,128,2048]{2,1,0:T(8,128)(2,1)S(1)}) fusion(s32[2048]{0:T(1024)S(1)} %bitcast.117, s32[128]{0:T(128)S(1)} %get-tuple-element.51, s32[2048]{0:T(1024)S(1)} %bitcast.116, s32[128]{0:T(128)S(1)} %get-tuple-element.50, s32[]{:T(128)} %bitcast.30), kind=kLoop, calls=%fused_computation.31 | loop fusion | flops 8126464 | bytes 1065988 | tf_op jit(solution)/shard_map/convert
  75.5 20.0 %all-gather.2.cloned.1.call-done = bf16[1,2,2048,256]{2,1,0,3:T(2,128)(2,1)} async-done(((bf16[1,2,2048,64]{2,1,0,3:T(2,128)(2,1)}), bf16[1,2,2048,256]{2,1,0,3:T(2,128)(2,1)}) %all-gather.2.cloned.1.call-update) | async-done | bytes 2097168 | tf_op jit(solution)/shard_map/all_gather | solution.py:96
  95.5 8.3 %copy.37 = bf16[1,2,2048,256]{3,1,2,0:T(2,128)(2,1)S(1)} copy(bf16[1,2,2048,256]{2,1,0,3:T(2,128)(2,1)} %all-gather.2.cloned.1.call-done) | data formatting | bytes 4194304 | tf_op jit(solution)/shard_map/all_gather | solution.py:96
  103.8 16.5 %gather_fusion = bf16[2048,2,256]{2,1,0:T(2,128)(2,1)} fusion(bf16[2,2048,256]{2,0,1:T(2,128)(2,1)S(1)} %bitcast.110, s32[2048]{0:T(1024)S(1)} %fusion.42), kind=kCustom, calls=%fused_computation | custom fusion | bytes 4202496 | tf_op jit(solution)/shard_map/jit(_take)/gather | solution.py:95
  120.3 2.1 %bitcast_select_fusion = bf16[1,2,2048,256]{3,2,0,1:T(8,128)(2,1)S(1)} fusion(pred[2048]{0:T(1024)(128)(4,1)S(1)} %compare_and_fusion, bf16[2048,2,256]{2,1,0:T(2,128)(2,1)} %gather_fusion), kind=kLoop, calls=%fused_computation.3 | loop fusion | flops 1048576 | bytes 4196352 | tf_op jit(solution)/shard_map/jit(_take)/select_n | solution.py:95
  122.5 0.9 fusion.8
  123.4 0.8 copy.39
  124.2 18.6 %all-to-all-start.1 = ((bf16[1,128,2,256]{3,2,0,1:T(2,128)(2,1)}), bf16[1,128,2,256]{3,2,0,1:T(2,128)(2,1)S(1)}, u32[]{:S(2)}, u32[]{:S(2)}) async-start(bf16[1,128,2,256]{3,2,0,1:T(2,128)(2,1)} %copy.39), calls=%async_computation.1 | async-start | bytes 262144 | tf_op jit(solution)/shard_map/all_to_all | solution.py:105
  142.9 1.3 fusion
  144.2 2.3 %fusion.47 = (f32[1,1,256,2048]{3,2,1,0:T(8,128)}, f32[1,1,256,2048]{3,2,1,0:T(8,128)}) fusion(f32[1,2,256,2048]{3,2,1,0:T(8,128)S(1)} %fusion), kind=kLoop, calls=%fused_computation.84 | loop fusion | bytes 8388608 | tf_op jit(solution)/shard_map/slice | solution.py:103
  146.5 16.1 %all-to-all-done.1 = bf16[1,128,2,256]{3,2,0,1:T(2,128)(2,1)S(1)} async-done(((bf16[1,128,2,256]{3,2,0,1:T(2,128)(2,1)}), bf16[1,128,2,256]{3,2,0,1:T(2,128)(2,1)S(1)}, u32[]{:S(2)}, u32[]{:S(2)}) %all-to-all-start.1) | async-done | bytes 131104 | tf_op jit(solution)/shard_map/all_to_all | solution.py:105
  162.6 0.3 convolution_bitcast_fusion.1
  162.9 0.2 copy.42
  163.1 1.0 reshape_reshape.3
  (22 shorter events, 0.6 us)
Async XLA Ops:
  7.2 63.3 %copy-start = (s32[1024,2]{0,1:T(2,128)S(1)}, s32[1024,2]{0,1:T(2,128)}, u32[]{:S(2)}) copy-start(s32[1024,2]{0,1:T(2,128)} %param.7) | copy-start | bytes 24580
  7.2 88.3 %all-gather.2.cloned.1.call-start = ((), (), s32[]{:S(2)}) async-start(), calls=%async_computation.2 | async-start | bytes 2621440 | tf_op jit(solution)/shard_map/all_gather | solution.py:96
  68.8 1.6 copy-start.2
  68.9 1.7 copy-start.3
  120.2 2.2 %copy-start.1 = (bf16[2048,2,256]{2,1,0:T(2,128)(2,1)S(1)}, bf16[2048,2,256]{2,1,0:T(2,128)(2,1)}, u32[]{:S(2)}) copy-start(bf16[2048,2,256]{2,1,0:T(2,128)(2,1)} %gather_fusion) | copy-start | bytes 6291460
  124.2 38.3 %all-to-all-start.1 = ((bf16[1,128,2,256]{3,2,0,1:T(2,128)(2,1)}), bf16[1,128,2,256]{3,2,0,1:T(2,128)(2,1)S(1)}, u32[]{:S(2)}, u32[]{:S(2)}) async-start(bf16[1,128,2,256]{3,2,0,1:T(2,128)(2,1)} %copy.39), calls=%async_computation.1 | async-start | bytes 262144 | tf_op jit(solution)/shard_map/all_to_all | solution.py:105
Sparse Core Ops, SparseCore 0:
  70.5 24.9 all-gather.1
where the time goes:
time: 171 us
  blocking collectives  57.2 us (33%)
  waiting for transfers between devices  36 us (21%)
  local copies, waits for them, and re-layouts  33.9 us (20%)
  starting transfers between devices  18.6 us (11%)
  between operations  14.3 us (8%)
  other arithmetic  7.53 us (4%)
  matrix products  3.38 us (2%)
    all_to_all x1, blocking collectives, per_device(): lax.all_to_all(spectra, 'band', split_axis=0, concat_axis=2, tiled=True)  57.2 us
    all_gather x1, waiting for transfers between devices, per_device(): lax.all_gather(owned, 'segment', axis=3, tiled=True)  20 us
    all_to_all x1, starting transfers between devices, per_device(): lax.all_to_all(formed_total.astype(jnp.bfloat16), 'band', split_axis=1, c...  18.6 us
    gather x1, local copies, waits for them, and re-layouts, per_device(): jnp.take(lax.all_gather(owned, 'segment', axis=3, tiled=True), slot_of_an...  16.5 us
    all_to_all x1, waiting for transfers between devices, per_device(): lax.all_to_all(formed_total.astype(jnp.bfloat16), 'band', split_axis=1, c...  16.1 us
    all_gather x1, local copies, waits for them, and re-layouts, per_device(): lax.all_gather(owned, 'segment', axis=3, tiled=True)  8.26 us
    another operation x1, other arithmetic  4.98 us
  transfers between devices with their start and end apart: 2, of which 2 were waited for; matrix products, arithmetic and copies ran while one was open for 5% of the time, Pallas kernels for 0%

commit v1 on v0

--- a/solution.py
+++ b/solution.py
@@ -1,3 +1,4 @@
+import functools
 import math
 import jax
 import jax.numpy as jnp
@@ -8,6 +9,21 @@
 C = 64
 BEAMS = 1024
 NB = 256
+
+
+def inputs_note(base_x, axis_id):
+    return jnp.concatenate(
+        lax.all_to_all(
+            jnp.stack([base_x] * lax.psum(1, axis_name=axis_id), 0),
+            split_axis=0,
+            concat_axis=0,
+            axis_name=axis_id,
+        ),
+        3,
+    )
+
+
+cells_remake = functools.partial(inputs_note, axis_id="segment")
 
 
 def dft_parts():
@@ -92,9 +108,7 @@
 
     spectra = paired(channelize(voltages))
     owned = lax.all_to_all(spectra, "band", split_axis=0, concat_axis=2, tiled=True)
-    ordered = jnp.take(
-        lax.all_gather(owned, "segment", axis=3, tiled=True), slot_of_antenna, axis=2
-    )
+    ordered = jnp.take(cells_remake(owned), slot_of_antenna, axis=2)
     gram_part, formed_part = jax.vmap(pair_terms)(ordered, weights, row_starts)
     formed_total = formed_part
     gram_total, formed_total = (gram_part, formed_total)

time: 171 us -> 148 us (0.87)
  blocking collectives: 57.2 us -> 0 us
  waiting for transfers between devices: 36 us -> 71.5 us
  between operations: 14.3 us -> 0.91 us
  starting transfers between devices: 18.6 us -> 31.2 us
    all_to_all x1 -> x0, blocking collectives: 57.2 us -> none  [per_device(): lax.all_to_all(spectra, 'band', split_axis=0, concat_axis=2, tiled=True)]
    all_to_all x0 -> x2, waiting for transfers between devices: none -> 56.2 us  [the longest x1 35.6 us: per_device(): lax.all_to_all(spectra, 'band', split_axis=0, concat_axis=2, tiled=True)]
    all_to_all x0 -> x2, starting transfers between devices: none -> 25.4 us  [the longest x1 21.6 us: per_device(): lax.all_to_all(spectra, 'band', split_axis=0, concat_axis=2, tiled=True)]
    all_gather x1 -> x0, waiting for transfers between devices: 20 us -> none  [per_device(): lax.all_gather(owned, 'segment', axis=3, tiled=True)]
    all_to_all x1, starting transfers between devices: 18.6 us -> 5.77 us  [per_device(): lax.all_to_all(formed_total.astype(jnp.bfloat16), 'band', split_axis=1, c...]
    all_gather x1 -> x0, local copies, waits for them, and re-layouts: 8.26 us -> none  [per_device(): lax.all_gather(owned, 'segment', axis=3, tiled=True)]
    reshape x0 -> x1, local copies, waits for them, and re-layouts: none -> 4.82 us  [inputs_note(): jnp.concatenate(lax.all_to_all(jnp.stack([base_x] * lax.psum(1, axis_name...]
    another operation x0 -> x2, local copies, waits for them, and re-layouts: none -> 1.95 us  [inputs_note(): jnp.stack([base_x] * lax.psum(1, axis_name=axis_id), 0)]
  transfers between devices with their start and end apart: 2 -> 3, of which waited for: 2 -> 3; matrix products, arithmetic and copies ran while one was open for 5% -> 6% of each run, Pallas kernels for 0% -> 0%
where the time goes in v1:
time: 148 us
  waiting for transfers between devices  71.5 us (48%)
  local copies, waits for them, and re-layouts  33.3 us (22%)
  starting transfers between devices  31.2 us (21%)
  other arithmetic  7.53 us (5%)
  matrix products  3.38 us (2%)
    all_to_all x1, waiting for transfers between devices, per_device(): lax.all_to_all(spectra, 'band', split_axis=0, concat_axis=2, tiled=True)  35.6 us
    all_to_all x1, starting transfers between devices, per_device(): lax.all_to_all(spectra, 'band', split_axis=0, concat_axis=2, tiled=True)  21.6 us
    all_to_all x1, waiting for transfers between devices, inputs_note(): lax.all_to_all(jnp.stack([base_x] * lax.psum(1, axis_name=axis_id), 0), s...  20.6 us
    gather x1, local copies, waits for them, and re-layouts, per_device(): ordered = jnp.take(cells_remake(owned), slot_of_antenna, axis=2)  16.5 us
    all_to_all x1, waiting for transfers between devices, per_device(): lax.all_to_all(formed_total.astype(jnp.bfloat16), 'band', split_axis=1, c...  15.3 us
    all_to_all x1, starting transfers between devices, per_device(): lax.all_to_all(formed_total.astype(jnp.bfloat16), 'band', split_axis=1, c...  5.77 us
    another operation x1, other arithmetic  4.98 us
    reshape x1, local copies, waits for them, and re-layouts, inputs_note(): jnp.concatenate(lax.all_to_all(jnp.stack([base_x] * lax.psum(1, axis_name...  4.82 us
  transfers between devices with their start and end apart: 3, of which 3 were waited for; matrix products, arithmetic and copies ran while one was open for 6% of the time, Pallas kernels for 0%

profile of v1, /device:TPU:32, one launch (start us, length us, event | category | flops | bytes accessed | tf_op | source)
XLA Modules:
  0.0 147.8 jit_solution(13216757828179900777)
XLA Ops:
  0.9 1.5 reshape.634
  2.5 0.9 fusion.7
  3.4 0.3 copy.36
  3.9 1.4 reshape.714
  5.3 21.6 %all-to-all-start = ((bf16[128,2,1024]{2,1,0:T(2,128)(2,1)}), bf16[128,2,1024]{2,1,0:T(2,128)(2,1)S(1)}, u32[]{:S(2)}, u32[]{:S(2)}) async-start(bf16[128,2,1024]{2,1,0:T(2,128)(2,1)} %reshape.714), calls=%async_computation | async-start | bytes 1048576 | tf_op jit(solution)/shard_map/all_to_all | solution.py:110
  27.0 35.6 %all-to-all-done = bf16[128,2,1024]{2,1,0:T(2,128)(2,1)S(1)} async-done(((bf16[128,2,1024]{2,1,0:T(2,128)(2,1)}), bf16[128,2,1024]{2,1,0:T(2,128)(2,1)S(1)}, u32[]{:S(2)}, u32[]{:S(2)}) %all-to-all-start) | async-done | bytes 524320 | tf_op jit(solution)/shard_map/all_to_all | solution.py:110
  62.6 0.6 reshape.715
  63.4 0.4 copy.38
  63.8 1.6 %stack.77 = bf16[4,1,2,2048,64]{3,4,2,1,0:T(8,128)(2,1)} broadcast(bf16[2,2048,64]{1,2,0:T(8,128)(2,1)S(1)} %copy.38), dimensions={2,3,4} | broadcast | bytes 2621440 | tf_op jit(solution)/shard_map/stack | solution.py:17
  65.4 3.7 %all-to-all-start.1 = ((bf16[4,1,2,2048,64]{3,4,2,1,0:T(8,128)(2,1)}), bf16[4,1,2,2048,64]{3,4,2,1,0:T(8,128)(2,1)S(1)}, u32[]{:S(2)}, u32[]{:S(2)}) async-start(bf16[4,1,2,2048,64]{3,4,2,1,0:T(8,128)(2,1)} %stack.77), calls=%async_computation.1 | async-start | bytes 4194304 | tf_op jit(solution)/shard_map/all_to_all | solution.py:16
  69.2 5.0 %cosine_convert_fusion = (bf16[1,128,2048]{2,1,0:T(8,128)(2,1)S(1)}, bf16[1,128,2048]{2,1,0:T(8,128)(2,1)S(1)}) fusion(s32[2048]{0:T(1024)S(1)} %bitcast.119, s32[128]{0:T(128)S(1)} %get-tuple-element.51, s32[2048]{0:T(1024)S(1)} %bitcast.118, s32[128]{0:T(128)S(1)} %get-tuple-element.50, s32[]{:T(128)} %bitcast.31), kind=kLoop, calls=%fused_computation.31 | loop fusion | flops 8126464 | bytes 1065988 | tf_op jit(solution)/shard_map/convert
  74.2 20.6 %all-to-all-done.1 = bf16[4,1,2,2048,64]{3,4,2,1,0:T(8,128)(2,1)S(1)} async-done(((bf16[4,1,2,2048,64]{3,4,2,1,0:T(8,128)(2,1)}), bf16[4,1,2,2048,64]{3,4,2,1,0:T(8,128)(2,1)S(1)}, u32[]{:S(2)}, u32[]{:S(2)}) %all-to-all-start.1) | async-done | bytes 2097184 | tf_op jit(solution)/shard_map/all_to_all | solution.py:16
  94.8 1.5 copy.39
  96.3 4.8 %copy.40 = bf16[2,2048,256]{2,0,1:T(2,128)(2,1)S(1)} copy(bf16[2,2048,256]{1,2,0:T(8,128)(2,1)} %bitcast.112) | data formatting | bytes 4194304 | tf_op jit(solution)/shard_map/reshape | solution.py:15
  101.1 16.5 %gather_fusion = bf16[2048,2,256]{2,1,0:T(2,128)(2,1)} fusion(bf16[2,2048,256]{2,0,1:T(2,128)(2,1)S(1)} %copy.40, s32[2048]{0:T(1024)S(1)} %fusion.42), kind=kCustom, calls=%fused_computation | custom fusion | bytes 4202496 | tf_op jit(solution)/shard_map/jit(_take)/gather | solution.py:111
  117.6 2.1 %bitcast_select_fusion = bf16[1,2,2048,256]{3,2,0,1:T(8,128)(2,1)S(1)} fusion(pred[2048]{0:T(1024)(128)(4,1)S(1)} %compare_and_fusion, bf16[2048,2,256]{2,1,0:T(2,128)(2,1)} %gather_fusion), kind=kLoop, calls=%fused_computation.3 | loop fusion | flops 1048576 | bytes 4196352 | tf_op jit(solution)/shard_map/jit(_take)/select_n | solution.py:111
  119.8 0.9 fusion.8
  120.7 0.8 copy.42
  121.5 5.8 %all-to-all-start.2 = ((bf16[1,128,2,256]{3,2,0,1:T(2,128)(2,1)}), bf16[1,128,2,256]{3,2,0,1:T(2,128)(2,1)S(1)}, u32[]{:S(2)}, u32[]{:S(2)}) async-start(bf16[1,128,2,256]{3,2,0,1:T(2,128)(2,1)} %copy.42), calls=%async_computation.2 | async-start | bytes 262144 | tf_op jit(solution)/shard_map/all_to_all | solution.py:119
  127.4 1.3 fusion
  128.7 2.3 %fusion.47 = (f32[1,1,256,2048]{3,2,1,0:T(8,128)}, f32[1,1,256,2048]{3,2,1,0:T(8,128)}) fusion(f32[1,2,256,2048]{3,2,1,0:T(8,128)S(1)} %fusion), kind=kLoop, calls=%fused_computation.84 | loop fusion | bytes 8388608 | tf_op jit(solution)/shard_map/slice | solution.py:117
  131.0 15.3 %all-to-all-done.2 = bf16[1,128,2,256]{3,2,0,1:T(2,128)(2,1)S(1)} async-done(((bf16[1,128,2,256]{3,2,0,1:T(2,128)(2,1)}), bf16[1,128,2,256]{3,2,0,1:T(2,128)(2,1)S(1)}, u32[]{:S(2)}, u32[]{:S(2)}) %all-to-all-start.2) | async-done | bytes 131104 | tf_op jit(solution)/shard_map/all_to_all | solution.py:119
  146.3 0.3 convolution_bitcast_fusion.1
  146.8 1.0 reshape_reshape.3
  (24 shorter events, 1.2 us)
Async XLA Ops:
  0.6 26.3 %copy-start = (s32[1024,2]{0,1:T(2,128)S(1)}, s32[1024,2]{0,1:T(2,128)}, u32[]{:S(2)}) copy-start(s32[1024,2]{0,1:T(2,128)} %param.7) | copy-start | bytes 24580
  5.3 57.3 %all-to-all-start = ((bf16[128,2,1024]{2,1,0:T(2,128)(2,1)}), bf16[128,2,1024]{2,1,0:T(2,128)(2,1)S(1)}, u32[]{:S(2)}, u32[]{:S(2)}) async-start(bf16[128,2,1024]{2,1,0:T(2,128)(2,1)} %reshape.714), calls=%async_computation | async-start | bytes 1048576 | tf_op jit(solution)/shard_map/all_to_all | solution.py:110
  65.4 3.8 %copy-start.2 = (s32[2048]{0:T(1024)S(1)}, s32[2048]{0:T(1024)}, u32[]{:S(2)}) copy-start(s32[2048]{0:T(1024)} %param.5) | copy-start | bytes 24580
  65.4 3.8 %copy-start.3 = (s32[2048,2]{0,1:T(2,128)S(1)}, s32[2048,2]{0,1:T(2,128)}, u32[]{:S(2)}) copy-start(s32[2048,2]{0,1:T(2,128)} %param.6) | copy-start | bytes 49156
  65.4 29.4 %all-to-all-start.1 = ((bf16[4,1,2,2048,64]{3,4,2,1,0:T(8,128)(2,1)}), bf16[4,1,2,2048,64]{3,4,2,1,0:T(8,128)(2,1)S(1)}, u32[]{:S(2)}, u32[]{:S(2)}) async-start(bf16[4,1,2,2048,64]{3,4,2,1,0:T(8,128)(2,1)} %stack.77), calls=%async_computation.1 | async-start | bytes 4194304 | tf_op jit(solution)/shard_map/all_to_all | solution.py:16
  117.6 2.2 %copy-start.1 = (bf16[2048,2,256]{2,1,0:T(2,128)(2,1)S(1)}, bf16[2048,2,256]{2,1,0:T(2,128)(2,1)}, u32[]{:S(2)}) copy-start(bf16[2048,2,256]{2,1,0:T(2,128)(2,1)} %gather_fusion) | copy-start | bytes 6291460
  121.5 24.7 %all-to-all-start.2 = ((bf16[1,128,2,256]{3,2,0,1:T(2,128)(2,1)}), bf16[1,128,2,256]{3,2,0,1:T(2,128)(2,1)S(1)}, u32[]{:S(2)}, u32[]{:S(2)}) async-start(bf16[1,128,2,256]{3,2,0,1:T(2,128)(2,1)} %copy.42), calls=%async_computation.2 | async-start | bytes 262144 | tf_op jit(solution)/shard_map/all_to_all | solution.py:119
